TPU v7x, 512 devices: a whole 4x8x8 slice. The times are simulated.
512 devices in a mesh: seg: 16 (over x, y_hi), pen: 32 (over y_lo, z, core).
Axes of the slice: x: 4, y: 8 (y_hi: 4, y_lo: 2; y = y_hi * 2 + y_lo), z: 8, core: 2. Of those that a mesh axis runs over, the one named last changes fastest.
Arguments:
- state: float32 [64, 384, 384], P('seg', 'pen'), may hold values from -6 to 6
- krylov: float32 [16, 64, 384, 384], P(None, 'seg', 'pen'), may hold values from -15 to 15
Outputs:
- residual: float32 [64, 384, 384], P('seg', 'pen')
- next_vector: float32 [64, 384, 384], P('seg', 'pen')
- hessenberg: float32 [17], replicated
All inputs are finite; a program needn't handle non-finite values.
Results may differ from a plain program's by a relative error of at most 0.0003.
Values sent between devices are 32-bit elements; how exact they have to be, the bound alone decides.
No kernel may reach another device: no remote copies, remote signals or barrier semaphores. Data moves between devices by JAX's collectives and lax.ppermute only.
A program may use at most 64 MiB of HBM per device.

v0:
```python
import functools

import jax
import jax.numpy as jnp
import numpy as np
from jax import lax
from jax.experimental import pallas as pl
from jax.experimental.pallas import tpu as pltpu
from jax.sharding import PartitionSpec as P


NX = 384
NZ = 384
PLANES = 4
STEPS = 2
KRY = 16
SEGS = 16
PEN = 32
CUT = NZ // PEN
TEAM = 8
WIDE = NZ // TEAM
TILE = 128
INTERPRET = False

time_step = 0.0003
viscosity = 0.0226


def pen_index(y, team, member):
    return 16 * y + 4 * team + member


TEAMS = [[pen_index(y, q, r) for y in range(2) for r in range(4)] for q in range(4)]
PEERS = [[pen_index(y, q, r) for q in range(4)] for y in range(2) for r in range(4)]


def row_order():
    rows = []
    for y in range(2):
        for r in range(4):
            for q in range(4):
                rows += [CUT * pen_index(y, q, r) + n for n in range(CUT)]
    return np.array(rows)


def split_table(table):
    high = np.asarray(table, dtype=np.float32).astype(jnp.bfloat16)
    low = np.asarray(table - high.astype(np.float64), dtype=np.float32).astype(jnp.bfloat16)
    return np.concatenate([high, low], 0)


@functools.lru_cache(None)
def tables():
    count = NX
    k = np.arange(count)
    angle = 2.0 * np.pi * (np.outer(k, k) % count) / count
    cas = np.cos(angle) + np.sin(angle)
    signed = np.where(k <= count // 2, k, k - count)
    slopes = np.where(k == count // 2, 0, signed)
    slope = slopes[:, None] * (np.cos(angle) - np.sin(angle))
    order = row_order()
    pick = np.ix_(order, order)
    return (
        split_table(np.concatenate([cas, slope], 1)),
        split_table(cas[pick]),
        split_table(slope[pick].T),
    )


def halves(value):
    high = value.astype(jnp.bfloat16)
    low = (value - high.astype(jnp.float32)).astype(jnp.bfloat16)
    return high, low


def mm(a, b):
    return jnp.dot(a, b, preferred_element_type=jnp.float32)


def times_table(value, table_ref):
    high, low = halves(value)
    upper, lower = table_ref[0:NX, :], table_ref[NX : 2 * NX, :]
    left = jnp.concatenate([high, low, high], 1)
    return mm(left, jnp.concatenate([upper, upper, lower], 0))


def few_times_table(value, table_ref):
    high, low = halves(value)
    n = value.shape[0]
    both = mm(jnp.concatenate([high, low], 0), table_ref[0:NX, 0:NX])
    return both[0:n] + both[n : 2 * n] + mm(high, table_ref[NX : 2 * NX, 0:NX])


def table_times(table_ref, value):
    high, low = halves(value)
    upper, lower = table_ref[0:NX, :], table_ref[NX : 2 * NX, :]
    left = jnp.concatenate([upper, upper, lower], 1)
    return mm(left, jnp.concatenate([high, low, high], 0))


def call(kernel, outs, operands, scratch=(), flops=0, moved=0, keep=True):
    vmem = pl.BlockSpec(memory_space=pltpu.VMEM)
    single = not isinstance(outs, (list, tuple))
    shapes = [outs] if single else list(outs)
    if not INTERPRET:
        operands = [pltpu.with_memory_space_constraint(x, pltpu.VMEM) for x in operands]
        shapes = [pltpu.VMEM(x.shape, x.dtype) for x in shapes] if keep else shapes
    results = pl.pallas_call(
        kernel,
        in_specs=[vmem] * len(operands),
        out_specs=[vmem] * len(shapes),
        out_shape=shapes,
        scratch_shapes=list(scratch),
        cost_estimate=pl.CostEstimate(flops=flops, bytes_accessed=moved, transcendentals=0),
        compiler_params=pltpu.CompilerParams(vmem_limit_bytes=24 << 20),
        interpret=INTERPRET,
    )(*operands)
    return results[0] if single else results


def f32(*shape):
    return jax.ShapeDtypeStruct(shape, jnp.float32)


def tile(t):
    return slice(TILE * t, TILE * (t + 1))


def gather_rows(state_ref, last_ref, out_ref):
    for q in range(4):
        for member, ref in enumerate((state_ref, last_ref)):
            for t in range(3):
                row = 36 * member + CUT * t
                out_ref[q, row : row + CUT, :] = ref[:, q, tile(t)]


def spread(fields, inverse_ref, table_ref, send_ref):
    base, tangent = fields
    inverse = inverse_ref[...]
    spectra = jnp.concatenate([base * inverse, tangent * inverse, base, tangent], 0)
    both = times_table(spectra, table_ref)
    values, slopes = both[:, 0:NX], both[:, NX : 2 * NX]
    for m in range(TEAM):
        cut = slice(WIDE * m, WIDE * (m + 1))
        v = [values[WIDE * k : WIDE * (k + 1), cut] for k in range(4)]
        s = [slopes[WIDE * k : WIDE * (k + 1), cut] for k in range(4)]
        parts = [v[0], v[1], s[2][:, :32], v[2], v[3], s[2][:, 32:], s[3][:, :16]]
        block = jnp.concatenate(parts + [s[0], s[1], s[3][:, 16:]], 1)
        for t in range(3):
            send_ref[m, WIDE * t : WIDE * (t + 1), :] = block[:, tile(t)]


def first_kernel(recv_ref, inverse_ref, table_ref, send_ref, fields_ref):
    for q in range(4):
        for member in range(2):
            for t in range(3):
                row = 36 * member + CUT * t
                fields_ref[member, CUT * q : CUT * (q + 1), tile(t)] = recv_ref[
                    q, row : row + CUT, :
                ]
    spread((fields_ref[0], fields_ref[1]), inverse_ref, table_ref, send_ref)


def grid_kernel(recv_ref, cas_ref, slope_ref, send_ref):
    tiles = [
        jnp.concatenate([recv_ref[m, WIDE * t : WIDE * (t + 1), :] for m in range(TEAM)], 0)
        for t in range(3)
    ]
    tiles.append(jnp.concatenate([x[:, 96:] for x in (tiles[0], tiles[1], tiles[2], tiles[0])], 1))
    along_z = table_times(slope_ref, jnp.concatenate(tiles[0:2], 1))
    along_x = table_times(cas_ref, jnp.concatenate(tiles[2:4], 1))
    psi_z, vort_z = along_z[:, tile(0)], along_z[:, tile(1)]
    psi_x, vort_x = along_x[:, tile(0)], along_x[:, tile(1)]
    base = lax.broadcasted_iota(jnp.int32, (NZ, TILE), 1) < WIDE

    def moved(x):
        return pltpu.roll(x, WIDE, 1)

    first = psi_x * jnp.where(base, vort_z, moved(vort_z))
    first = first - psi_z * jnp.where(base, vort_x, moved(vort_x))
    second = moved(psi_x) * vort_z - moved(psi_z) * vort_x
    total = first + jnp.where(base, 0.0, second)
    modes = table_times(cas_ref, total)
    for m in range(TEAM):
        send_ref[m] = modes[WIDE * m : WIDE * (m + 1), :]


def advanced(recv_ref, fields_ref, damping_ref, table_ref):
    lines = [
        jnp.concatenate(
            [recv_ref[m, :, WIDE * member : WIDE * (member + 1)] for m in range(TEAM)], 1
        )
        for member in range(2)
    ]
    forcing = few_times_table(jnp.concatenate(lines, 0), table_ref)
    scale = time_step / (NX * NZ)
    damping = damping_ref[...]
    return [
        (fields_ref[member] + scale * forcing[WIDE * member : WIDE * (member + 1)]) * damping
        for member in range(2)
    ]


def middle_kernel(
    recv_ref, old_ref, damping_ref, inverse_ref, table_ref, send_ref, fields_ref
):
    fields = advanced(recv_ref, old_ref, damping_ref, table_ref)
    fields_ref[0] = fields[0]
    fields_ref[1] = fields[1]
    spread(fields, inverse_ref, table_ref, send_ref)


def last_kernel(recv_ref, old_ref, damping_ref, table_ref, out_ref):
    fields = advanced(recv_ref, old_ref, damping_ref, table_ref)
    for member in range(2):
        for q in range(4):
            for t in range(3):
                row = 36 * member + CUT * t
                out_ref[q, row : row + CUT, :] = fields[member][
                    CUT * q : CUT * (q + 1), tile(t)
                ]


def row_sums(value):
    ones = jnp.ones((8, TILE), jnp.bfloat16)
    first = value.astype(jnp.bfloat16)
    rest = value - first.astype(jnp.float32)
    second = rest.astype(jnp.bfloat16)
    third = (rest - second.astype(jnp.float32)).astype(jnp.bfloat16)
    dims = (((1,), (1,)), ((), ()))
    total = jnp.zeros((8, value.shape[0]), jnp.float32)
    for part in (third, second, first):
        total = total + lax.dot_general(ones, part, dims, preferred_element_type=jnp.float32)
    return total


def fold(value):
    return jnp.sum(value, axis=0, keepdims=True)


def fold(value):
    line = value[:, tile(0)] + value[:, tile(1)] + value[:, tile(2)]
    return jnp.sum(line, axis=0, keepdims=True)


def gram_kernel(kry_ref, out_ref, keep):
    for a in range(0, KRY, 4):
        for b in range(0, a + 1, 4):

            def step(g, sums):
                left = [kry_ref[a + i, g] for i in range(4)]
                right = [kry_ref[b + j, g] for j in range(4)]
                pairs = [(i, j) for i in range(4) for j in range(4)]
                return tuple(sums[4 * i + j] + left[i] * right[j] for i, j in pairs)

            zero = jnp.zeros((PLANES, NX), jnp.float32)
            sums = lax.fori_loop(0, CUT, step, (zero,) * 16)
            for i in range(4):
                for j in range(4):
                    line = fold(sums[4 * i + j])
                    keep[KRY * (a + i) + b + j : KRY * (a + i) + b + j + 1, :] = line
                    if a != b:
                        keep[KRY * (b + j) + a + i : KRY * (b + j) + a + i + 1, :] = line
    packed = row_sums(keep[...])
    row = lax.broadcasted_iota(jnp.int32, (8, TILE), 0)
    out_ref[...] = jnp.where(
        row == 1, packed[:, 0:TILE], jnp.where(row == 2, packed[:, TILE : 2 * TILE], 0.0)
    )


def place(planes_ref, out_ref):
    for p in range(PLANES):
        for t in range(3):
            out_ref[:, p, tile(t)] = planes_ref[p, CUT * t : CUT * (t + 1), :]


def dots_kernel(planes_ref, kry_ref, gram_ref, image_ref, out_ref, keep):
    place(planes_ref, image_ref)
    image = image_ref[...] - kry_ref[KRY - 1]
    image_ref[...] = image
    keep[...] = jnp.zeros_like(keep)
    for k in range(KRY):
        keep[k : k + 1, :] = fold(jnp.sum(kry_ref[k] * image, axis=0))
    keep[KRY : KRY + 1, :] = fold(jnp.sum(image * image, axis=0))
    packed = row_sums(keep[...])
    row = lax.broadcasted_iota(jnp.int32, (8, TILE), 0)
    sums = jnp.where(row == 0, packed, gram_ref[...])
    for m in range(out_ref.shape[0]):
        out_ref[m] = sums


def finish_kernel(
    sums_ref, kry_ref, image_ref, state_ref, planes_ref, residual_ref, next_ref, hess_ref
):
    place(planes_ref, residual_ref)
    residual_ref[...] = residual_ref[...] - state_ref[...]
    total = float(SEGS * PLANES * NZ * NX)
    sums = sums_ref[0]
    for s in range(1, sums_ref.shape[0]):
        sums = sums + sums_ref[s]
    sums = sums / total
    coeffs = [sums[0:1, k : k + 1] for k in range(KRY)]
    remain = image_ref[...]
    for k in range(KRY):
        remain = remain - coeffs[k] * kry_ref[k]
    lane = lax.broadcasted_iota(jnp.int32, (1, TILE), 1)
    inner = jnp.zeros((1, TILE), jnp.float32)
    outer = [inner, inner]
    for k in range(KRY):
        inner = jnp.where(lane % KRY == k, coeffs[k], inner)
        half, block = k // 8, k % 8
        outer[half] = jnp.where(lane // KRY == block, coeffs[k], outer[half])
    line = jnp.where(lane < KRY, sums[0:1] * sums[0:1], 0.0)
    quadratic = inner * (outer[0] * sums[1:2] + outer[1] * sums[2:3]) - 2.0 * line
    squared = sums[0:1, KRY : KRY + 1] + jnp.sum(quadratic, axis=1, keepdims=True)
    norm = jnp.sqrt(jnp.maximum(squared, 0.0) + 1e-06)
    next_ref[...] = remain / norm
    hess = jnp.where(lane == KRY, norm, sums[0:1])
    hess_ref[...] = hess[0, : KRY + 1]


def reduce_groups(segs):
    def number(place, inner):
        seg, y = place
        return seg * PEN + 16 * y + inner

    places = [(seg, y) for seg in range(segs) for y in range(2)]
    columns = [[number(place, inner) for inner in range(16)] for place in places]
    planes = [[number(place, inner) for place in places] for inner in range(16)]
    return columns, planes


def body(state, krylov):
    pen = lax.axis_index("pen")
    segs = lax.axis_size("seg")
    numbers = np.arange(NX)
    signed = np.where(numbers <= NX // 2, numbers, numbers - NX).astype(np.float32)
    steps = np.arange(WIDE)
    rows = CUT * (16 * (pen // 16) + pen % 4) + (4 * CUT * (steps // CUT) + steps % CUT)
    mode = jnp.where(rows <= NZ // 2, rows, rows - NZ).astype(jnp.float32)
    ksquare = mode[:, None] ** 2 + signed[None, :] ** 2
    inverse = jnp.where(ksquare > 0, 1.0 / jnp.where(ksquare > 0, ksquare, 1.0), 0.0)
    damping = 1.0 / (1.0 + time_step * viscosity * ksquare)
    table, cas_z, slope_z = [jnp.asarray(t) for t in tables()]
    state_f = state.transpose(1, 0, 2)
    kry_f = krylov.transpose(0, 2, 1, 3)
    exchange = functools.partial(
        lax.all_to_all, axis_name="pen", split_axis=0, concat_axis=0, tiled=True
    )
    everywhere = functools.partial(
        lax.all_to_all, axis_name=("seg", "pen"), split_axis=0, concat_axis=0, tiled=True
    )
    columns, planes = reduce_groups(segs)
    ring = [(s, (s + 1) % segs) for s in range(segs)]

    whole = pl.BlockSpec((CUT, PLANES, NX), lambda i: (0, 0, 0))
    last = pl.BlockSpec((None, CUT, PLANES, NX), lambda i: (KRY - 1, 0, 0, 0))
    inputs = [state_f, kry_f]
    if not INTERPRET:
        inputs = [pltpu.with_memory_space_constraint(x, pltpu.HBM) for x in inputs]
    packed = pl.pallas_call(
        gather_rows,
        grid=(1,),
        in_specs=[whole, last],
        out_specs=pl.BlockSpec((4, 72, TILE), lambda i: (0, 0, 0)),
        out_shape=f32(4, 72, TILE),
        compiler_params=pltpu.CompilerParams(vmem_limit_bytes=24 << 20),
        interpret=INTERPRET,
    )(*inputs)
    packed = exchange(packed, axis_index_groups=PEERS)
    both = (f32(TEAM, 144, TILE), f32(2, WIDE, NX))
    send, fields = call(
        first_kernel, both, [packed, inverse, table], flops=700_000_000, moved=3_000_000
    )
    for repeat in range(STEPS):
        recv = exchange(send, axis_index_groups=TEAMS)
        modes = call(
            grid_kernel,
            f32(TEAM, WIDE, TILE),
            [recv, cas_z, slope_z],
            flops=900_000_000,
            moved=2_500_000,
        )
        recv = exchange(modes, axis_index_groups=TEAMS)
        if repeat < STEPS - 1:
            send, fields = call(
                middle_kernel,
                both,
                [recv, fields, damping, inverse, table],
                flops=900_000_000,
                moved=3_000_000,
            )
    ends = call(
        last_kernel,
        f32(4, 72, TILE),
        [recv, fields, damping, table],
        flops=200_000_000,
        moved=1_500_000,
    )
    ends = exchange(ends, axis_index_groups=PEERS)
    tangent = lax.ppermute(ends[:, 36:72], "seg", ring)
    gram = call(
        gram_kernel,
        f32(8, TILE),
        [kry_f],
        [pltpu.VMEM((KRY * KRY, TILE), jnp.float32)],
        flops=10_000_000,
        moved=1_300_000,
    )
    base, gram = lax.optimization_barrier((ends[:, 0:36], gram))
    base = lax.ppermute(base, "seg", ring)
    image, partial = call(
        dots_kernel,
        [f32(CUT, PLANES, NX), f32(16, 8, TILE)],
        [tangent, kry_f, gram],
        [pltpu.VMEM((TILE, TILE), jnp.float32)],
        flops=1_000_000,
        moved=1_300_000,
    )
    sums = everywhere(partial, axis_index_groups=columns)
    sums = jnp.sum(sums, axis=0)
    sums, base = lax.optimization_barrier((sums, base))
    sums = jnp.broadcast_to(sums[None], (2 * segs, 8, TILE))
    sums = everywhere(sums, axis_index_groups=planes)
    residual, vector, hess = call(
        finish_kernel,
        [f32(CUT, PLANES, NX)] * 2 + [f32(KRY + 1)],
        [sums, kry_f, image, state_f, base],
        flops=1_000_000,
        moved=1_500_000,
        keep=False,
    )
    return (residual.transpose(1, 0, 2), vector.transpose(1, 0, 2), hess)


def solution(mesh):
    return jax.shard_map(
        body,
        mesh=mesh,
        in_specs=(P("seg", "pen", None), P(None, "seg", "pen", None)),
        out_specs=(P("seg", "pen", None), P("seg", "pen", None), P()),
        check_vma=False,
    )
```

profile of v0, /device:TPU:8, one launch (start us, length us, event | category | flops | bytes accessed | tf_op | source)
XLA Modules:
  0.0 126.1 jit_solution(9186128301584847976)
XLA Ops:
  0.6 0.0 copy-start.6
  0.6 0.0 copy-start.5
  0.7 0.0 copy-start.1
  0.7 1.8 %shard_map.94 = f32[4,72,128]{2,1,0:T(8,128)} custom-call(f32[12,4,384]{2,1,0:T(4,128)} %bitcast.8, f32[16,12,4,384]{3,2,1,0:T(4,128)} %bitcast.4), custom_call_target="tpu_custom_call" | custom-call | tf_op jit(solution)/shard_map/pallas_call | solution.py:361
  2.4 10.3 %all-to-all-start = ((f32[4,72,128]{2,1,0:T(8,128)}), f32[4,72,128]{2,1,0:T(8,128)S(1)}, u32[]{:S(2)}, u32[]{:S(2)}) async-start(f32[4,72,128]{2,1,0:T(8,128)} %shard_map.94), calls=%async_computation | async-start | bytes 294912 | tf_op jit(solution)/shard_map/all_to_all | solution.py:370
  12.7 0.0 copy-done.6
  12.7 0.0 copy-done.5
  12.8 0.1 fusion.3
  12.9 9.5 %all-to-all-done.recv_ref = f32[4,72,128]{2,1,0:T(8,128)S(1)} async-done(((f32[4,72,128]{2,1,0:T(8,128)}), f32[4,72,128]{2,1,0:T(8,128)S(1)}, u32[]{:S(2)}, u32[]{:S(2)}) %all-to-all-start) | async-done | bytes 147488 | tf_op jit(solution)/shard_map/all_to_all | solution.py:370
  22.3 0.0 copy-done.1
  22.3 1.0 shard_map.95
  23.3 0.0 copy-start.3
  23.3 0.0 copy-start.4
  23.3 12.2 %all_to_all.40.recv_ref = f32[8,144,128]{2,1,0:T(8,128)S(1)} all-to-all(f32[8,144,128]{2,1,0:T(8,128)S(1)} %get-tuple-element.16), channel_id=1, replica_groups={{0,1,2,3,16,17,18,19},{4,5,6,7,20,21,22,23},{8,9,10,11,24,25,26,27},{12..., dimensions={0} | all-to-all | bytes 1179648 | tf_op jit(solution)/shard_map/all_to_all | solution.py:376
  35.5 0.0 copy-done.3
  35.5 0.0 copy-done.4
  35.5 1.4 %shard_map.96 = f32[8,48,128]{2,1,0:T(8,128)S(1)} custom-call(f32[8,144,128]{2,1,0:T(8,128)S(1)} %all_to_all.40.recv_ref, bf16[768,384]{1,0:T(8,128)(2,1)S(1)} %copy-done.3, bf16[768,384]{1,0:T(8,128)(2,1)S(1)} %copy-done.4), custom_call_target="tpu_custom_call" | custom-call | flops 900000000 | bytes 2500000 | tf_op jit(solution)/shard_map/pallas_call | solution.py:108
  36.9 8.5 %all_to_all.41.recv_ref = f32[8,48,128]{2,1,0:T(8,128)S(1)} all-to-all(f32[8,48,128]{2,1,0:T(8,128)S(1)} %shard_map.96), channel_id=1, replica_groups={{0,1,2,3,16,17,18,19},{4,5,6,7,20,21,22,23},{8,9,10,11,24,25,26,27},{12..., dimensions={0} | all-to-all | bytes 393216 | tf_op jit(solution)/shard_map/all_to_all | solution.py:384
  45.5 1.3 %shard_map.97 = (f32[8,144,128]{2,1,0:T(8,128)S(1)}, f32[2,48,384]{2,1,0:T(8,128)S(1)}) custom-call(f32[8,48,128]{2,1,0:T(8,128)S(1)} %all_to_all.41.recv_ref, f32[2,48,384]{2,1,0:T(8,128)S(1)} %get-tuple-element.17.old_ref, f32[48,384]{1,0:T(8,128)S(1)} %get-tuple-element.31.damping_ref, f32[48,384]{1,0:T(8,128)S(1)} %get-tuple-element.32.inverse_ref, ...), custom_call_target="tpu_custom_call" | custom-call | flops 900000000 | bytes 3000000 | tf_op jit(solution)/shard_map/pallas_call | solution.py:108
  46.8 12.3 %all_to_all.42.recv_ref = f32[8,144,128]{2,1,0:T(8,128)S(1)} all-to-all(f32[8,144,128]{2,1,0:T(8,128)S(1)} %get-tuple-element.18), channel_id=1, replica_groups={{0,1,2,3,16,17,18,19},{4,5,6,7,20,21,22,23},{8,9,10,11,24,25,26,27},{12..., dimensions={0} | all-to-all | bytes 1179648 | tf_op jit(solution)/shard_map/all_to_all | solution.py:376
  59.0 1.4 %shard_map.98 = f32[8,48,128]{2,1,0:T(8,128)S(1)} custom-call(f32[8,144,128]{2,1,0:T(8,128)S(1)} %all_to_all.42.recv_ref, bf16[768,384]{1,0:T(8,128)(2,1)S(1)} %copy-done.3, bf16[768,384]{1,0:T(8,128)(2,1)S(1)} %copy-done.4), custom_call_target="tpu_custom_call" | custom-call | flops 900000000 | bytes 2500000 | tf_op jit(solution)/shard_map/pallas_call | solution.py:108
  60.5 8.5 %all_to_all.43.recv_ref = f32[8,48,128]{2,1,0:T(8,128)S(1)} all-to-all(f32[8,48,128]{2,1,0:T(8,128)S(1)} %shard_map.98), channel_id=1, replica_groups={{0,1,2,3,16,17,18,19},{4,5,6,7,20,21,22,23},{8,9,10,11,24,25,26,27},{12..., dimensions={0} | all-to-all | bytes 393216 | tf_op jit(solution)/shard_map/all_to_all | solution.py:384
  69.0 0.0 copy-start
  69.0 0.4 shard_map.99
  69.4 11.8 %all_to_all.44 = f32[4,72,128]{2,1,0:T(8,128)S(1)} all-to-all(f32[4,72,128]{2,1,0:T(8,128)S(1)} %shard_map.99), channel_id=1, replica_groups={{0,4,8,12},{1,5,9,13},{2,6,10,14},{3,7,11,15},{16,20,24,28},{17,21,25,2..., dimensions={0} | all-to-all | bytes 294912 | tf_op jit(solution)/shard_map/all_to_all | solution.py:400
  81.2 4.5 %collective-permute-start = (f32[4,36,128]{2,1,0:T(8,128)S(1)}, f32[4,36,128]{2,1,0:T(8,128)S(1)}, u32[]{:S(2)}, u32[]{:S(2)}) collective-permute-start(f32[4,36,128]{2,1,0:T(8,128)S(1)} %get-tuple-element.30), channel_id=1, source_target_pairs={{0,32},{32,64},{64,96},{96,128},{128,160},{160,192},{192,224},{224... | collective-permute-start | bytes 221192 | tf_op jit(solution)/shard_map/ppermute | solution.py:401
  85.7 0.0 copy-done
  85.7 2.3 %shard_map.100.gram_ref = f32[8,128]{1,0:T(8,128)S(1)} custom-call(f32[16,12,4,384]{3,2,1,0:T(4,128)S(1)} %bitcast.5), custom_call_target="tpu_custom_call" | custom-call | flops 10000000 | bytes 1300000 | tf_op jit(solution)/shard_map/pallas_call | solution.py:108
  88.0 0.0 copy-start.2
  88.0 3.8 %collective-permute-done.planes_ref = f32[4,36,128]{2,1,0:T(8,128)S(1)} collective-permute-done((f32[4,36,128]{2,1,0:T(8,128)S(1)}, f32[4,36,128]{2,1,0:T(8,128)S(1)}, u32[]{:S(2)}, u32[]{:S(2)}) %collective-permute-start) | collective-permute-done | bytes 73760 | tf_op jit(solution)/shard_map/ppermute | solution.py:401
  91.8 1.2 shard_map.101
  93.0 3.5 %all-to-all-start.6 = ((f32[16,8,128]{2,1,0:T(8,128)}), f32[16,8,128]{2,1,0:T(8,128)S(1)}, u32[]{:S(2)}, u32[]{:S(2)}) async-start(f32[16,8,128]{2,1,0:T(8,128)} %get-tuple-element.21), calls=%async_computation.6 | async-start | bytes 131072 | tf_op jit(solution)/shard_map/all_to_all | solution.py:420
  96.5 2.1 %collective-permute-start.1 = (f32[4,36,128]{2,1,0:T(8,128)S(1)}, f32[4,36,128]{2,1,0:T(8,128)S(1)}, u32[]{:S(2)}, u32[]{:S(2)}) collective-permute-start(f32[4,36,128]{2,1,0:T(8,128)S(1)} %get-tuple-element.22), channel_id=1, source_target_pairs={{0,32},{32,64},{64,96},{96,128},{128,160},{160,192},{192,224},{224... | collective-permute-start | bytes 221192 | tf_op jit(solution)/shard_map/ppermute | solution.py:411
  98.6 5.6 %all-to-all-done.6 = f32[16,8,128]{2,1,0:T(8,128)S(1)} async-done(((f32[16,8,128]{2,1,0:T(8,128)}), f32[16,8,128]{2,1,0:T(8,128)S(1)}, u32[]{:S(2)}, u32[]{:S(2)}) %all-to-all-start.6) | async-done | bytes 65568 | tf_op jit(solution)/shard_map/all_to_all | solution.py:420
  104.3 4.0 %collective-permute-done.1.planes_ref = f32[4,36,128]{2,1,0:T(8,128)S(1)} collective-permute-done((f32[4,36,128]{2,1,0:T(8,128)S(1)}, f32[4,36,128]{2,1,0:T(8,128)S(1)}, u32[]{:S(2)}, u32[]{:S(2)}) %collective-permute-start.1) | collective-permute-done | bytes 73760 | tf_op jit(solution)/shard_map/ppermute | solution.py:411
  108.4 16.7 %all_to_all.45.sums_ref = f32[32,8,128]{2,1,0:T(8,128)S(1)} all-to-all(f32[32,8,128]{2,1,0:T(8,128)S(1)} %broadcast_in_dim.5), channel_id=1, replica_groups={{0,16,32,48,64,80,96,112,128,144,160,176,192,208,224,240,256,272,288,30..., dimensions={0} | all-to-all | bytes 262144 | tf_op jit(solution)/shard_map/all_to_all | solution.py:424
  125.0 0.0 copy-done.2
  125.0 1.0 shard_map.102
  (4 shorter events, 0.0 us)
Async XLA Ops:
  0.6 12.1 %copy-start.6 = (s32[48]{0:T(128)S(1)}, s32[48]{0:T(128)}, u32[]{:S(2)}) copy-start(s32[48]{0:T(128)} %constant.57.clone) | copy-start | bytes 580
  0.6 12.1 %copy-start.5 = (f32[384]{0:T(512)S(1)}, f32[384]{0:T(512)}, u32[]{:S(2)}) copy-start(f32[384]{0:T(512)} %constant.64) | copy-start | bytes 4612
  0.7 21.7 %copy-start.1 = (bf16[768,768]{1,0:T(8,128)(2,1)S(1)}, bf16[768,768]{1,0:T(8,128)(2,1)}, u32[]{:S(2)}) copy-start(bf16[768,768]{1,0:T(8,128)(2,1)} %constant.59.clone.table_ref) | copy-start | bytes 3538948
  2.4 19.9 %all-to-all-start = ((f32[4,72,128]{2,1,0:T(8,128)}), f32[4,72,128]{2,1,0:T(8,128)S(1)}, u32[]{:S(2)}, u32[]{:S(2)}) async-start(f32[4,72,128]{2,1,0:T(8,128)} %shard_map.94), calls=%async_computation | async-start | bytes 294912 | tf_op jit(solution)/shard_map/all_to_all | solution.py:370
  23.3 12.2 %copy-start.3 = (bf16[768,384]{1,0:T(8,128)(2,1)S(1)}, bf16[768,384]{1,0:T(8,128)(2,1)}, u32[]{:S(2)}) copy-start(bf16[768,384]{1,0:T(8,128)(2,1)} %constant.60.clone.cas_ref) | copy-start | bytes 1769476
  23.3 12.2 %copy-start.4 = (bf16[768,384]{1,0:T(8,128)(2,1)S(1)}, bf16[768,384]{1,0:T(8,128)(2,1)}, u32[]{:S(2)}) copy-start(bf16[768,384]{1,0:T(8,128)(2,1)} %constant.61.clone.slope_ref) | copy-start | bytes 1769476
  69.0 16.7 %copy-start = (f32[16,4,12,384]{3,1,2,0:T(4,128)S(1)}, f32[16,4,12,384]{3,1,2,0:T(4,128)}, u32[]{:S(2)}) copy-start(f32[16,4,12,384]{3,1,2,0:T(4,128)} %param.8) | copy-start | bytes 3538948
  81.2 10.7 %collective-permute-start = (f32[4,36,128]{2,1,0:T(8,128)S(1)}, f32[4,36,128]{2,1,0:T(8,128)S(1)}, u32[]{:S(2)}, u32[]{:S(2)}) collective-permute-start(f32[4,36,128]{2,1,0:T(8,128)S(1)} %get-tuple-element.30), channel_id=1, source_target_pairs={{0,32},{32,64},{64,96},{96,128},{128,160},{160,192},{192,224},{224... | collective-permute-start | bytes 221192 | tf_op jit(solution)/shard_map/ppermute | solution.py:401
  88.0 37.0 %copy-start.2 = (f32[4,12,384]{2,0,1:T(4,128)S(1)}, f32[4,12,384]{2,0,1:T(4,128)}, u32[]{:S(2)}) copy-start(f32[4,12,384]{2,0,1:T(4,128)} %param.7) | copy-start | bytes 221188
  93.0 11.3 %all-to-all-start.6 = ((f32[16,8,128]{2,1,0:T(8,128)}), f32[16,8,128]{2,1,0:T(8,128)S(1)}, u32[]{:S(2)}, u32[]{:S(2)}) async-start(f32[16,8,128]{2,1,0:T(8,128)} %get-tuple-element.21), calls=%async_computation.6 | async-start | bytes 131072 | tf_op jit(solution)/shard_map/all_to_all | solution.py:420
  96.5 11.8 %collective-permute-start.1 = (f32[4,36,128]{2,1,0:T(8,128)S(1)}, f32[4,36,128]{2,1,0:T(8,128)S(1)}, u32[]{:S(2)}, u32[]{:S(2)}) collective-permute-start(f32[4,36,128]{2,1,0:T(8,128)S(1)} %get-tuple-element.22), channel_id=1, source_target_pairs={{0,32},{32,64},{64,96},{96,128},{128,160},{160,192},{192,224},{224... | collective-permute-start | bytes 221192 | tf_op jit(solution)/shard_map/ppermute | solution.py:411
where the time goes:
time: 127 us; the launch traced here: 126 us
  blocking collectives  69.9 us (55%)
  waiting for transfers between devices  23 us (18%)
  starting transfers between devices  20.4 us (16%)
  Pallas kernels  11.8 us (9%)
    all_to_all x2, blocking collectives, body(): recv = exchange(send, axis_index_groups=TEAMS)  24.5 us
    all_to_all x2, blocking collectives, body(): recv = exchange(modes, axis_index_groups=TEAMS)  17 us
    all_to_all x1, blocking collectives, body(): sums = everywhere(sums, axis_index_groups=planes)  16.7 us
    all_to_all x1, blocking collectives, body(): ends = exchange(ends, axis_index_groups=PEERS)  11.8 us
    all_to_all x1, starting transfers between devices, body(): packed = exchange(packed, axis_index_groups=PEERS)  10.3 us
    pallas_call x8, Pallas kernels, call(): pl.pallas_call(kernel, in_specs=[vmem] * len(operands), out_specs=[vmem]...  10 us
    all_to_all x1, waiting for transfers between devices, body(): packed = exchange(packed, axis_index_groups=PEERS)  9.47 us
    all_to_all x1, waiting for transfers between devices, body(): sums = everywhere(partial, axis_index_groups=columns)  5.64 us
  transfers between devices with their start and end apart: 4, of which 4 were waited for; matrix products, arithmetic and copies ran while one was open for 0% of the time, Pallas kernels for 2%

commit v1 on v0

--- a/solution.py
+++ b/solution.py
@@ -271,7 +271,8 @@
 def place(planes_ref, out_ref):
     for p in range(PLANES):
         for t in range(3):
-            out_ref[:, p, tile(t)] = planes_ref[p, CUT * t : CUT * (t + 1), :]
+            row = 36 * p + CUT * t
+            out_ref[:, p, tile(t)] = planes_ref[row : row + CUT, :]
 
 
 def dots_kernel(planes_ref, kry_ref, gram_ref, image_ref, out_ref, keep):
@@ -398,7 +399,7 @@
         moved=1_500_000,
     )
     ends = exchange(ends, axis_index_groups=PEERS)
-    tangent = lax.ppermute(ends[:, 36:72], "seg", ring)
+    tangent = lax.ppermute(ends[:, 36:72].reshape(144, TILE), "seg", ring)
     gram = call(
         gram_kernel,
         f32(8, TILE),
@@ -407,7 +408,7 @@
         flops=10_000_000,
         moved=1_300_000,
     )
-    base, gram = lax.optimization_barrier((ends[:, 0:36], gram))
+    base, gram = lax.optimization_barrier((ends[:, 0:36].reshape(144, TILE), gram))
     base = lax.ppermute(base, "seg", ring)
     image, partial = call(
         dots_kernel,

time: 127 us -> 126 us (level)
  no operation moved by 1% of the time
where the time goes in v1:
time: 126 us
  blocking collectives  69.6 us (55%)
  waiting for transfers between devices  22.7 us (18%)
  starting transfers between devices  20.3 us (16%)
  Pallas kernels  11.8 us (9%)
    all_to_all x2, blocking collectives, body(): recv = exchange(send, axis_index_groups=TEAMS)  24.5 us
    all_to_all x2, blocking collectives, body(): recv = exchange(modes, axis_index_groups=TEAMS)  17 us
    all_to_all x1, blocking collectives, body(): sums = everywhere(sums, axis_index_groups=planes)  16.4 us
    all_to_all x1, blocking collectives, body(): ends = exchange(ends, axis_index_groups=PEERS)  11.8 us
    all_to_all x1, starting transfers between devices, body(): packed = exchange(packed, axis_index_groups=PEERS)  10.3 us
    pallas_call x8, Pallas kernels, call(): pl.pallas_call(kernel, in_specs=[vmem] * len(operands), out_specs=[vmem]...  10 us
    all_to_all x1, waiting for transfers between devices, body(): packed = exchange(packed, axis_index_groups=PEERS)  9.47 us
    all_to_all x1, waiting for transfers between devices, body(): sums = everywhere(partial, axis_index_groups=columns)  5.73 us
  transfers between devices with their start and end apart: 4, of which 4 were waited for; matrix products, arithmetic and copies ran while one was open for 0% of the time, Pallas kernels for 2%

profile of v1, /device:TPU:8, one launch (start us, length us, event | category | flops | bytes accessed | tf_op | source)
XLA Modules:
  0.0 125.5 jit_solution(2955105451156246383)
XLA Ops:
  0.6 0.0 copy-start.6
  0.6 0.0 copy-start.5
  0.7 0.0 copy-start.1
  0.7 1.8 %shard_map.94 = f32[4,72,128]{2,1,0:T(8,128)} custom-call(f32[12,4,384]{2,1,0:T(4,128)} %bitcast.8, f32[16,12,4,384]{3,2,1,0:T(4,128)} %bitcast.4), custom_call_target="tpu_custom_call" | custom-call | tf_op jit(solution)/shard_map/pallas_call | solution.py:362
  2.4 10.3 %all-to-all-start = ((f32[4,72,128]{2,1,0:T(8,128)}), f32[4,72,128]{2,1,0:T(8,128)S(1)}, u32[]{:S(2)}, u32[]{:S(2)}) async-start(f32[4,72,128]{2,1,0:T(8,128)} %shard_map.94), calls=%async_computation | async-start | bytes 294912 | tf_op jit(solution)/shard_map/all_to_all | solution.py:371
  12.7 0.0 copy-done.6
  12.7 0.0 copy-done.5
  12.8 0.1 fusion.3
  12.9 9.5 %all-to-all-done.recv_ref = f32[4,72,128]{2,1,0:T(8,128)S(1)} async-done(((f32[4,72,128]{2,1,0:T(8,128)}), f32[4,72,128]{2,1,0:T(8,128)S(1)}, u32[]{:S(2)}, u32[]{:S(2)}) %all-to-all-start) | async-done | bytes 147488 | tf_op jit(solution)/shard_map/all_to_all | solution.py:371
  22.3 0.0 copy-done.1
  22.3 1.0 shard_map.95
  23.3 0.0 copy-start.3
  23.3 0.0 copy-start.4
  23.3 12.2 %all_to_all.40.recv_ref = f32[8,144,128]{2,1,0:T(8,128)S(1)} all-to-all(f32[8,144,128]{2,1,0:T(8,128)S(1)} %get-tuple-element.16), channel_id=1, replica_groups={{0,1,2,3,16,17,18,19},{4,5,6,7,20,21,22,23},{8,9,10,11,24,25,26,27},{12..., dimensions={0} | all-to-all | bytes 1179648 | tf_op jit(solution)/shard_map/all_to_all | solution.py:377
  35.5 0.0 copy-done.3
  35.5 0.0 copy-done.4
  35.5 1.4 %shard_map.96 = f32[8,48,128]{2,1,0:T(8,128)S(1)} custom-call(f32[8,144,128]{2,1,0:T(8,128)S(1)} %all_to_all.40.recv_ref, bf16[768,384]{1,0:T(8,128)(2,1)S(1)} %copy-done.3, bf16[768,384]{1,0:T(8,128)(2,1)S(1)} %copy-done.4), custom_call_target="tpu_custom_call" | custom-call | flops 900000000 | bytes 2500000 | tf_op jit(solution)/shard_map/pallas_call | solution.py:108
  36.9 8.5 %all_to_all.41.recv_ref = f32[8,48,128]{2,1,0:T(8,128)S(1)} all-to-all(f32[8,48,128]{2,1,0:T(8,128)S(1)} %shard_map.96), channel_id=1, replica_groups={{0,1,2,3,16,17,18,19},{4,5,6,7,20,21,22,23},{8,9,10,11,24,25,26,27},{12..., dimensions={0} | all-to-all | bytes 393216 | tf_op jit(solution)/shard_map/all_to_all | solution.py:385
  45.5 1.3 %shard_map.97 = (f32[8,144,128]{2,1,0:T(8,128)S(1)}, f32[2,48,384]{2,1,0:T(8,128)S(1)}) custom-call(f32[8,48,128]{2,1,0:T(8,128)S(1)} %all_to_all.41.recv_ref, f32[2,48,384]{2,1,0:T(8,128)S(1)} %get-tuple-element.17.old_ref, f32[48,384]{1,0:T(8,128)S(1)} %get-tuple-element.31.damping_ref, f32[48,384]{1,0:T(8,128)S(1)} %get-tuple-element.32.inverse_ref, ...), custom_call_target="tpu_custom_call" | custom-call | flops 900000000 | bytes 3000000 | tf_op jit(solution)/shard_map/pallas_call | solution.py:108
  46.8 12.3 %all_to_all.42.recv_ref = f32[8,144,128]{2,1,0:T(8,128)S(1)} all-to-all(f32[8,144,128]{2,1,0:T(8,128)S(1)} %get-tuple-element.18), channel_id=1, replica_groups={{0,1,2,3,16,17,18,19},{4,5,6,7,20,21,22,23},{8,9,10,11,24,25,26,27},{12..., dimensions={0} | all-to-all | bytes 1179648 | tf_op jit(solution)/shard_map/all_to_all | solution.py:377
  59.0 1.4 %shard_map.98 = f32[8,48,128]{2,1,0:T(8,128)S(1)} custom-call(f32[8,144,128]{2,1,0:T(8,128)S(1)} %all_to_all.42.recv_ref, bf16[768,384]{1,0:T(8,128)(2,1)S(1)} %copy-done.3, bf16[768,384]{1,0:T(8,128)(2,1)S(1)} %copy-done.4), custom_call_target="tpu_custom_call" | custom-call | flops 900000000 | bytes 2500000 | tf_op jit(solution)/shard_map/pallas_call | solution.py:108
  60.5 8.5 %all_to_all.43.recv_ref = f32[8,48,128]{2,1,0:T(8,128)S(1)} all-to-all(f32[8,48,128]{2,1,0:T(8,128)S(1)} %shard_map.98), channel_id=1, replica_groups={{0,1,2,3,16,17,18,19},{4,5,6,7,20,21,22,23},{8,9,10,11,24,25,26,27},{12..., dimensions={0} | all-to-all | bytes 393216 | tf_op jit(solution)/shard_map/all_to_all | solution.py:385
  69.0 0.0 copy-start
  69.0 0.4 shard_map.99
  69.4 11.8 %all_to_all.44 = f32[4,72,128]{2,1,0:T(8,128)S(1)} all-to-all(f32[4,72,128]{2,1,0:T(8,128)S(1)} %shard_map.99), channel_id=1, replica_groups={{0,4,8,12},{1,5,9,13},{2,6,10,14},{3,7,11,15},{16,20,24,28},{17,21,25,2..., dimensions={0} | all-to-all | bytes 294912 | tf_op jit(solution)/shard_map/all_to_all | solution.py:401
  81.2 4.5 %collective-permute-start = (f32[144,128]{1,0:T(8,128)S(1)}, f32[144,128]{1,0:T(8,128)S(1)}, u32[]{:S(2)}, u32[]{:S(2)}) collective-permute-start(f32[144,128]{1,0:T(8,128)S(1)} %reshape.15), channel_id=1, source_target_pairs={{0,32},{32,64},{64,96},{96,128},{128,160},{160,192},{192,224},{224... | collective-permute-start | bytes 221192 | tf_op jit(solution)/shard_map/ppermute | solution.py:402
  85.7 0.0 copy-done
  85.7 2.3 %shard_map.100.gram_ref = f32[8,128]{1,0:T(8,128)S(1)} custom-call(f32[16,12,4,384]{3,2,1,0:T(4,128)S(1)} %bitcast.5), custom_call_target="tpu_custom_call" | custom-call | flops 10000000 | bytes 1300000 | tf_op jit(solution)/shard_map/pallas_call | solution.py:108
  88.0 0.0 copy-start.2
  88.0 0.1 reshape.16
  88.1 3.7 %collective-permute-done.planes_ref = f32[144,128]{1,0:T(8,128)S(1)} collective-permute-done((f32[144,128]{1,0:T(8,128)S(1)}, f32[144,128]{1,0:T(8,128)S(1)}, u32[]{:S(2)}, u32[]{:S(2)}) %collective-permute-start) | collective-permute-done | bytes 73760 | tf_op jit(solution)/shard_map/ppermute | solution.py:402
  91.8 1.2 shard_map.101
  92.9 3.5 %all-to-all-start.6 = ((f32[16,8,128]{2,1,0:T(8,128)}), f32[16,8,128]{2,1,0:T(8,128)S(1)}, u32[]{:S(2)}, u32[]{:S(2)}) async-start(f32[16,8,128]{2,1,0:T(8,128)} %get-tuple-element.21), calls=%async_computation.6 | async-start | bytes 131072 | tf_op jit(solution)/shard_map/all_to_all | solution.py:421
  96.4 2.0 %collective-permute-start.1 = (f32[144,128]{1,0:T(8,128)S(1)}, f32[144,128]{1,0:T(8,128)S(1)}, u32[]{:S(2)}, u32[]{:S(2)}) collective-permute-start(f32[144,128]{1,0:T(8,128)S(1)} %reshape.16), channel_id=1, source_target_pairs={{0,32},{32,64},{64,96},{96,128},{128,160},{160,192},{192,224},{224... | collective-permute-start | bytes 221192 | tf_op jit(solution)/shard_map/ppermute | solution.py:412
  98.5 5.7 %all-to-all-done.6 = f32[16,8,128]{2,1,0:T(8,128)S(1)} async-done(((f32[16,8,128]{2,1,0:T(8,128)}), f32[16,8,128]{2,1,0:T(8,128)S(1)}, u32[]{:S(2)}, u32[]{:S(2)}) %all-to-all-start.6) | async-done | bytes 65568 | tf_op jit(solution)/shard_map/all_to_all | solution.py:421
  104.2 3.9 %collective-permute-done.1.planes_ref = f32[144,128]{1,0:T(8,128)S(1)} collective-permute-done((f32[144,128]{1,0:T(8,128)S(1)}, f32[144,128]{1,0:T(8,128)S(1)}, u32[]{:S(2)}, u32[]{:S(2)}) %collective-permute-start.1) | collective-permute-done | bytes 73760 | tf_op jit(solution)/shard_map/ppermute | solution.py:412
  108.1 16.4 %all_to_all.45.sums_ref = f32[32,8,128]{2,1,0:T(8,128)S(1)} all-to-all(f32[32,8,128]{2,1,0:T(8,128)S(1)} %broadcast_in_dim.5), channel_id=1, replica_groups={{0,16,32,48,64,80,96,112,128,144,160,176,192,208,224,240,256,272,288,30..., dimensions={0} | all-to-all | bytes 262144 | tf_op jit(solution)/shard_map/all_to_all | solution.py:425
  124.5 0.0 copy-done.2
  124.5 1.0 shard_map.102
  (5 shorter events, 0.1 us)
Async XLA Ops:
  0.6 12.1 %copy-start.6 = (s32[48]{0:T(128)S(1)}, s32[48]{0:T(128)}, u32[]{:S(2)}) copy-start(s32[48]{0:T(128)} %constant.57.clone) | copy-start | bytes 580
  0.6 12.1 %copy-start.5 = (f32[384]{0:T(512)S(1)}, f32[384]{0:T(512)}, u32[]{:S(2)}) copy-start(f32[384]{0:T(512)} %constant.64) | copy-start | bytes 4612
  0.7 21.7 %copy-start.1 = (bf16[768,768]{1,0:T(8,128)(2,1)S(1)}, bf16[768,768]{1,0:T(8,128)(2,1)}, u32[]{:S(2)}) copy-start(bf16[768,768]{1,0:T(8,128)(2,1)} %constant.59.clone.table_ref) | copy-start | bytes 3538948
  2.4 19.9 %all-to-all-start = ((f32[4,72,128]{2,1,0:T(8,128)}), f32[4,72,128]{2,1,0:T(8,128)S(1)}, u32[]{:S(2)}, u32[]{:S(2)}) async-start(f32[4,72,128]{2,1,0:T(8,128)} %shard_map.94), calls=%async_computation | async-start | bytes 294912 | tf_op jit(solution)/shard_map/all_to_all | solution.py:371
  23.3 12.2 %copy-start.3 = (bf16[768,384]{1,0:T(8,128)(2,1)S(1)}, bf16[768,384]{1,0:T(8,128)(2,1)}, u32[]{:S(2)}) copy-start(bf16[768,384]{1,0:T(8,128)(2,1)} %constant.60.clone.cas_ref) | copy-start | bytes 1769476
  23.3 12.2 %copy-start.4 = (bf16[768,384]{1,0:T(8,128)(2,1)S(1)}, bf16[768,384]{1,0:T(8,128)(2,1)}, u32[]{:S(2)}) copy-start(bf16[768,384]{1,0:T(8,128)(2,1)} %constant.61.clone.slope_ref) | copy-start | bytes 1769476
  69.0 16.7 %copy-start = (f32[16,4,12,384]{3,1,2,0:T(4,128)S(1)}, f32[16,4,12,384]{3,1,2,0:T(4,128)}, u32[]{:S(2)}) copy-start(f32[16,4,12,384]{3,1,2,0:T(4,128)} %param.8) | copy-start | bytes 3538948
  81.2 10.6 %collective-permute-start = (f32[144,128]{1,0:T(8,128)S(1)}, f32[144,128]{1,0:T(8,128)S(1)}, u32[]{:S(2)}, u32[]{:S(2)}) collective-permute-start(f32[144,128]{1,0:T(8,128)S(1)} %reshape.15), channel_id=1, source_target_pairs={{0,32},{32,64},{64,96},{96,128},{128,160},{160,192},{192,224},{224... | collective-permute-start | bytes 221192 | tf_op jit(solution)/shard_map/ppermute | solution.py:402
  88.0 36.5 %copy-start.2 = (f32[4,12,384]{2,0,1:T(4,128)S(1)}, f32[4,12,384]{2,0,1:T(4,128)}, u32[]{:S(2)}) copy-start(f32[4,12,384]{2,0,1:T(4,128)} %param.7) | copy-start | bytes 221188
  92.9 11.3 %all-to-all-start.6 = ((f32[16,8,128]{2,1,0:T(8,128)}), f32[16,8,128]{2,1,0:T(8,128)S(1)}, u32[]{:S(2)}, u32[]{:S(2)}) async-start(f32[16,8,128]{2,1,0:T(8,128)} %get-tuple-element.21), calls=%async_computation.6 | async-start | bytes 131072 | tf_op jit(solution)/shard_map/all_to_all | solution.py:421
  96.4 11.6 %collective-permute-start.1 = (f32[144,128]{1,0:T(8,128)S(1)}, f32[144,128]{1,0:T(8,128)S(1)}, u32[]{:S(2)}, u32[]{:S(2)}) collective-permute-start(f32[144,128]{1,0:T(8,128)S(1)} %reshape.16), channel_id=1, source_target_pairs={{0,32},{32,64},{64,96},{96,128},{128,160},{160,192},{192,224},{224... | collective-permute-start | bytes 221192 | tf_op jit(solution)/shard_map/ppermute | solution.py:412

commit v2 on v1

--- a/solution.py
+++ b/solution.py
@@ -126,12 +126,19 @@
     return slice(TILE * t, TILE * (t + 1))
 
 
-def gather_rows(state_ref, last_ref, out_ref):
-    for q in range(4):
-        for member, ref in enumerate((state_ref, last_ref)):
+def gather_rows(state_ref, kry_ref, out_ref, state_rows, last_rows, arrived):
+    copies = [
+        pltpu.make_async_copy(state_ref, state_rows, arrived.at[0]),
+        pltpu.make_async_copy(kry_ref.at[KRY - 1], last_rows, arrived.at[1]),
+    ]
+    for copy in copies:
+        copy.start()
+    for member, rows in enumerate((state_rows, last_rows)):
+        copies[member].wait()
+        for q in range(4):
             for t in range(3):
                 row = 36 * member + CUT * t
-                out_ref[q, row : row + CUT, :] = ref[:, q, tile(t)]
+                out_ref[q, row : row + CUT, :] = rows[:, q, tile(t)]
 
 
 def spread(fields, inverse_ref, table_ref, send_ref):
@@ -354,16 +361,18 @@
     columns, planes = reduce_groups(segs)
     ring = [(s, (s + 1) % segs) for s in range(segs)]
 
-    whole = pl.BlockSpec((CUT, PLANES, NX), lambda i: (0, 0, 0))
-    last = pl.BlockSpec((None, CUT, PLANES, NX), lambda i: (KRY - 1, 0, 0, 0))
     inputs = [state_f, kry_f]
     if not INTERPRET:
         inputs = [pltpu.with_memory_space_constraint(x, pltpu.HBM) for x in inputs]
     packed = pl.pallas_call(
         gather_rows,
-        grid=(1,),
-        in_specs=[whole, last],
-        out_specs=pl.BlockSpec((4, 72, TILE), lambda i: (0, 0, 0)),
+        in_specs=[pl.BlockSpec(memory_space=pl.ANY)] * 2,
+        out_specs=pl.BlockSpec(memory_space=pltpu.VMEM),
+        scratch_shapes=[
+            pltpu.VMEM((CUT, PLANES, NX), jnp.float32),
+            pltpu.VMEM((CUT, PLANES, NX), jnp.float32),
+            pltpu.SemaphoreType.DMA((2,)),
+        ],
         out_shape=f32(4, 72, TILE),
         compiler_params=pltpu.CompilerParams(vmem_limit_bytes=24 << 20),
         interpret=INTERPRET,

time: 126 us -> 126 us (level)
  no operation moved by 1% of the time
where the time goes in v2:
time: 126 us
  blocking collectives  69.7 us (55%)
  waiting for transfers between devices  22.7 us (18%)
  starting transfers between devices  20.3 us (16%)
  Pallas kernels  11.8 us (9%)
    all_to_all x2, blocking collectives, body(): recv = exchange(send, axis_index_groups=TEAMS)  24.5 us
    all_to_all x2, blocking collectives, body(): recv = exchange(modes, axis_index_groups=TEAMS)  17 us
    all_to_all x1, blocking collectives, body(): sums = everywhere(sums, axis_index_groups=planes)  16.4 us
    all_to_all x1, blocking collectives, body(): ends = exchange(ends, axis_index_groups=PEERS)  11.8 us
    all_to_all x1, starting transfers between devices, body(): packed = exchange(packed, axis_index_groups=PEERS)  10.3 us
    pallas_call x8, Pallas kernels, call(): pl.pallas_call(kernel, in_specs=[vmem] * len(operands), out_specs=[vmem]...  10 us
    all_to_all x1, waiting for transfers between devices, body(): packed = exchange(packed, axis_index_groups=PEERS)  9.47 us
    all_to_all x1, waiting for transfers between devices, body(): sums = everywhere(partial, axis_index_groups=columns)  5.73 us
  transfers between devices with their start and end apart: 4, of which 4 were waited for; matrix products, arithmetic and copies ran while one was open for 0% of the time, Pallas kernels for 2%

profile of v2, /device:TPU:8, one launch (start us, length us, event | category | flops | bytes accessed | tf_op | source)
XLA Modules:
  0.0 125.5 jit_solution(5345374298883823171)
XLA Ops:
  0.6 0.0 copy-start.6
  0.6 0.0 copy-start.5
  0.7 0.0 copy-start.1
  0.7 1.8 %shard_map.94 = f32[4,72,128]{2,1,0:T(8,128)} custom-call(f32[12,4,384]{2,1,0:T(4,128)} %bitcast.8, f32[16,12,4,384]{3,2,1,0:T(4,128)} %bitcast.4), custom_call_target="tpu_custom_call" | custom-call | tf_op jit(solution)/shard_map/pallas_call | solution.py:367
  2.4 10.3 %all-to-all-start = ((f32[4,72,128]{2,1,0:T(8,128)}), f32[4,72,128]{2,1,0:T(8,128)S(1)}, u32[]{:S(2)}, u32[]{:S(2)}) async-start(f32[4,72,128]{2,1,0:T(8,128)} %shard_map.94), calls=%async_computation | async-start | bytes 294912 | tf_op jit(solution)/shard_map/all_to_all | solution.py:380
  12.7 0.0 copy-done.6
  12.8 0.0 copy-done.5
  12.8 0.1 fusion.3
  12.9 9.5 %all-to-all-done.recv_ref = f32[4,72,128]{2,1,0:T(8,128)S(1)} async-done(((f32[4,72,128]{2,1,0:T(8,128)}), f32[4,72,128]{2,1,0:T(8,128)S(1)}, u32[]{:S(2)}, u32[]{:S(2)}) %all-to-all-start) | async-done | bytes 147488 | tf_op jit(solution)/shard_map/all_to_all | solution.py:380
  22.3 0.0 copy-done.1
  22.3 0.9 shard_map.95
  23.3 0.0 copy-start.3
  23.3 0.0 copy-start.4
  23.3 12.2 %all_to_all.40.recv_ref = f32[8,144,128]{2,1,0:T(8,128)S(1)} all-to-all(f32[8,144,128]{2,1,0:T(8,128)S(1)} %get-tuple-element.16), channel_id=1, replica_groups={{0,1,2,3,16,17,18,19},{4,5,6,7,20,21,22,23},{8,9,10,11,24,25,26,27},{12..., dimensions={0} | all-to-all | bytes 1179648 | tf_op jit(solution)/shard_map/all_to_all | solution.py:386
  35.5 0.0 copy-done.3
  35.5 0.0 copy-done.4
  35.5 1.4 %shard_map.96 = f32[8,48,128]{2,1,0:T(8,128)S(1)} custom-call(f32[8,144,128]{2,1,0:T(8,128)S(1)} %all_to_all.40.recv_ref, bf16[768,384]{1,0:T(8,128)(2,1)S(1)} %copy-done.3, bf16[768,384]{1,0:T(8,128)(2,1)S(1)} %copy-done.4), custom_call_target="tpu_custom_call" | custom-call | flops 900000000 | bytes 2500000 | tf_op jit(solution)/shard_map/pallas_call | solution.py:108
  36.9 8.5 %all_to_all.41.recv_ref = f32[8,48,128]{2,1,0:T(8,128)S(1)} all-to-all(f32[8,48,128]{2,1,0:T(8,128)S(1)} %shard_map.96), channel_id=1, replica_groups={{0,1,2,3,16,17,18,19},{4,5,6,7,20,21,22,23},{8,9,10,11,24,25,26,27},{12..., dimensions={0} | all-to-all | bytes 393216 | tf_op jit(solution)/shard_map/all_to_all | solution.py:394
  45.5 1.3 %shard_map.97 = (f32[8,144,128]{2,1,0:T(8,128)S(1)}, f32[2,48,384]{2,1,0:T(8,128)S(1)}) custom-call(f32[8,48,128]{2,1,0:T(8,128)S(1)} %all_to_all.41.recv_ref, f32[2,48,384]{2,1,0:T(8,128)S(1)} %get-tuple-element.17.old_ref, f32[48,384]{1,0:T(8,128)S(1)} %get-tuple-element.31.damping_ref, f32[48,384]{1,0:T(8,128)S(1)} %get-tuple-element.32.inverse_ref, ...), custom_call_target="tpu_custom_call" | custom-call | flops 900000000 | bytes 3000000 | tf_op jit(solution)/shard_map/pallas_call | solution.py:108
  46.8 12.3 %all_to_all.42.recv_ref = f32[8,144,128]{2,1,0:T(8,128)S(1)} all-to-all(f32[8,144,128]{2,1,0:T(8,128)S(1)} %get-tuple-element.18), channel_id=1, replica_groups={{0,1,2,3,16,17,18,19},{4,5,6,7,20,21,22,23},{8,9,10,11,24,25,26,27},{12..., dimensions={0} | all-to-all | bytes 1179648 | tf_op jit(solution)/shard_map/all_to_all | solution.py:386
  59.1 1.4 %shard_map.98 = f32[8,48,128]{2,1,0:T(8,128)S(1)} custom-call(f32[8,144,128]{2,1,0:T(8,128)S(1)} %all_to_all.42.recv_ref, bf16[768,384]{1,0:T(8,128)(2,1)S(1)} %copy-done.3, bf16[768,384]{1,0:T(8,128)(2,1)S(1)} %copy-done.4), custom_call_target="tpu_custom_call" | custom-call | flops 900000000 | bytes 2500000 | tf_op jit(solution)/shard_map/pallas_call | solution.py:108
  60.5 8.5 %all_to_all.43.recv_ref = f32[8,48,128]{2,1,0:T(8,128)S(1)} all-to-all(f32[8,48,128]{2,1,0:T(8,128)S(1)} %shard_map.98), channel_id=1, replica_groups={{0,1,2,3,16,17,18,19},{4,5,6,7,20,21,22,23},{8,9,10,11,24,25,26,27},{12..., dimensions={0} | all-to-all | bytes 393216 | tf_op jit(solution)/shard_map/all_to_all | solution.py:394
  69.0 0.0 copy-start
  69.0 0.4 shard_map.99
  69.4 11.8 %all_to_all.44 = f32[4,72,128]{2,1,0:T(8,128)S(1)} all-to-all(f32[4,72,128]{2,1,0:T(8,128)S(1)} %shard_map.99), channel_id=1, replica_groups={{0,4,8,12},{1,5,9,13},{2,6,10,14},{3,7,11,15},{16,20,24,28},{17,21,25,2..., dimensions={0} | all-to-all | bytes 294912 | tf_op jit(solution)/shard_map/all_to_all | solution.py:410
  81.2 4.5 %collective-permute-start = (f32[144,128]{1,0:T(8,128)S(1)}, f32[144,128]{1,0:T(8,128)S(1)}, u32[]{:S(2)}, u32[]{:S(2)}) collective-permute-start(f32[144,128]{1,0:T(8,128)S(1)} %reshape.15), channel_id=1, source_target_pairs={{0,32},{32,64},{64,96},{96,128},{128,160},{160,192},{192,224},{224... | collective-permute-start | bytes 221192 | tf_op jit(solution)/shard_map/ppermute | solution.py:411
  85.7 0.0 copy-done
  85.7 2.3 %shard_map.100.gram_ref = f32[8,128]{1,0:T(8,128)S(1)} custom-call(f32[16,12,4,384]{3,2,1,0:T(4,128)S(1)} %bitcast.5), custom_call_target="tpu_custom_call" | custom-call | flops 10000000 | bytes 1300000 | tf_op jit(solution)/shard_map/pallas_call | solution.py:108
  88.0 0.0 copy-start.2
  88.0 0.1 reshape.16
  88.1 3.7 %collective-permute-done.planes_ref = f32[144,128]{1,0:T(8,128)S(1)} collective-permute-done((f32[144,128]{1,0:T(8,128)S(1)}, f32[144,128]{1,0:T(8,128)S(1)}, u32[]{:S(2)}, u32[]{:S(2)}) %collective-permute-start) | collective-permute-done | bytes 73760 | tf_op jit(solution)/shard_map/ppermute | solution.py:411
  91.8 1.2 shard_map.101
  92.9 3.5 %all-to-all-start.6 = ((f32[16,8,128]{2,1,0:T(8,128)}), f32[16,8,128]{2,1,0:T(8,128)S(1)}, u32[]{:S(2)}, u32[]{:S(2)}) async-start(f32[16,8,128]{2,1,0:T(8,128)} %get-tuple-element.21), calls=%async_computation.6 | async-start | bytes 131072 | tf_op jit(solution)/shard_map/all_to_all | solution.py:430
  96.4 2.0 %collective-permute-start.1 = (f32[144,128]{1,0:T(8,128)S(1)}, f32[144,128]{1,0:T(8,128)S(1)}, u32[]{:S(2)}, u32[]{:S(2)}) collective-permute-start(f32[144,128]{1,0:T(8,128)S(1)} %reshape.16), channel_id=1, source_target_pairs={{0,32},{32,64},{64,96},{96,128},{128,160},{160,192},{192,224},{224... | collective-permute-start | bytes 221192 | tf_op jit(solution)/shard_map/ppermute | solution.py:421
  98.5 5.7 %all-to-all-done.6 = f32[16,8,128]{2,1,0:T(8,128)S(1)} async-done(((f32[16,8,128]{2,1,0:T(8,128)}), f32[16,8,128]{2,1,0:T(8,128)S(1)}, u32[]{:S(2)}, u32[]{:S(2)}) %all-to-all-start.6) | async-done | bytes 65568 | tf_op jit(solution)/shard_map/all_to_all | solution.py:430
  104.2 3.9 %collective-permute-done.1.planes_ref = f32[144,128]{1,0:T(8,128)S(1)} collective-permute-done((f32[144,128]{1,0:T(8,128)S(1)}, f32[144,128]{1,0:T(8,128)S(1)}, u32[]{:S(2)}, u32[]{:S(2)}) %collective-permute-start.1) | collective-permute-done | bytes 73760 | tf_op jit(solution)/shard_map/ppermute | solution.py:421
  108.1 16.4 %all_to_all.45.sums_ref = f32[32,8,128]{2,1,0:T(8,128)S(1)} all-to-all(f32[32,8,128]{2,1,0:T(8,128)S(1)} %broadcast_in_dim.5), channel_id=1, replica_groups={{0,16,32,48,64,80,96,112,128,144,160,176,192,208,224,240,256,272,288,30..., dimensions={0} | all-to-all | bytes 262144 | tf_op jit(solution)/shard_map/all_to_all | solution.py:434
  124.5 0.0 copy-done.2
  124.5 1.0 shard_map.102
  (5 shorter events, 0.1 us)
Async XLA Ops:
  0.6 12.1 %copy-start.6 = (s32[48]{0:T(128)S(1)}, s32[48]{0:T(128)}, u32[]{:S(2)}) copy-start(s32[48]{0:T(128)} %constant.57.clone) | copy-start | bytes 580
  0.6 12.1 %copy-start.5 = (f32[384]{0:T(512)S(1)}, f32[384]{0:T(512)}, u32[]{:S(2)}) copy-start(f32[384]{0:T(512)} %constant.64) | copy-start | bytes 4612
  0.7 21.7 %copy-start.1 = (bf16[768,768]{1,0:T(8,128)(2,1)S(1)}, bf16[768,768]{1,0:T(8,128)(2,1)}, u32[]{:S(2)}) copy-start(bf16[768,768]{1,0:T(8,128)(2,1)} %constant.59.clone.table_ref) | copy-start | bytes 3538948
  2.4 19.9 %all-to-all-start = ((f32[4,72,128]{2,1,0:T(8,128)}), f32[4,72,128]{2,1,0:T(8,128)S(1)}, u32[]{:S(2)}, u32[]{:S(2)}) async-start(f32[4,72,128]{2,1,0:T(8,128)} %shard_map.94), calls=%async_computation | async-start | bytes 294912 | tf_op jit(solution)/shard_map/all_to_all | solution.py:380
  23.3 12.2 %copy-start.3 = (bf16[768,384]{1,0:T(8,128)(2,1)S(1)}, bf16[768,384]{1,0:T(8,128)(2,1)}, u32[]{:S(2)}) copy-start(bf16[768,384]{1,0:T(8,128)(2,1)} %constant.60.clone.cas_ref) | copy-start | bytes 1769476
  23.3 12.2 %copy-start.4 = (bf16[768,384]{1,0:T(8,128)(2,1)S(1)}, bf16[768,384]{1,0:T(8,128)(2,1)}, u32[]{:S(2)}) copy-start(bf16[768,384]{1,0:T(8,128)(2,1)} %constant.61.clone.slope_ref) | copy-start | bytes 1769476
  69.0 16.7 %copy-start = (f32[16,4,12,384]{3,1,2,0:T(4,128)S(1)}, f32[16,4,12,384]{3,1,2,0:T(4,128)}, u32[]{:S(2)}) copy-start(f32[16,4,12,384]{3,1,2,0:T(4,128)} %param.8) | copy-start | bytes 3538948
  81.2 10.6 %collective-permute-start = (f32[144,128]{1,0:T(8,128)S(1)}, f32[144,128]{1,0:T(8,128)S(1)}, u32[]{:S(2)}, u32[]{:S(2)}) collective-permute-start(f32[144,128]{1,0:T(8,128)S(1)} %reshape.15), channel_id=1, source_target_pairs={{0,32},{32,64},{64,96},{96,128},{128,160},{160,192},{192,224},{224... | collective-permute-start | bytes 221192 | tf_op jit(solution)/shard_map/ppermute | solution.py:411
  88.0 36.5 %copy-start.2 = (f32[4,12,384]{2,0,1:T(4,128)S(1)}, f32[4,12,384]{2,0,1:T(4,128)}, u32[]{:S(2)}) copy-start(f32[4,12,384]{2,0,1:T(4,128)} %param.7) | copy-start | bytes 221188
  92.9 11.3 %all-to-all-start.6 = ((f32[16,8,128]{2,1,0:T(8,128)}), f32[16,8,128]{2,1,0:T(8,128)S(1)}, u32[]{:S(2)}, u32[]{:S(2)}) async-start(f32[16,8,128]{2,1,0:T(8,128)} %get-tuple-element.21), calls=%async_computation.6 | async-start | bytes 131072 | tf_op jit(solution)/shard_map/all_to_all | solution.py:430
  96.4 11.6 %collective-permute-start.1 = (f32[144,128]{1,0:T(8,128)S(1)}, f32[144,128]{1,0:T(8,128)S(1)}, u32[]{:S(2)}, u32[]{:S(2)}) collective-permute-start(f32[144,128]{1,0:T(8,128)S(1)} %reshape.16), channel_id=1, source_target_pairs={{0,32},{32,64},{64,96},{96,128},{128,160},{160,192},{192,224},{224... | collective-permute-start | bytes 221192 | tf_op jit(solution)/shard_map/ppermute | solution.py:421

commit v3 on v1

--- a/solution.py
+++ b/solution.py
@@ -254,7 +254,7 @@
                 return tuple(sums[4 * i + j] + left[i] * right[j] for i, j in pairs)
 
             zero = jnp.zeros((PLANES, NX), jnp.float32)
-            sums = lax.fori_loop(0, CUT, step, (zero,) * 16)
+            sums = lax.fori_loop(0, CUT, step, (zero,) * 16, unroll=3)
             for i in range(4):
                 for j in range(4):
                     line = fold(sums[4 * i + j])
@@ -334,9 +334,9 @@
 def body(state, krylov):
     pen = lax.axis_index("pen")
     segs = lax.axis_size("seg")
-    numbers = np.arange(NX)
-    signed = np.where(numbers <= NX // 2, numbers, numbers - NX).astype(np.float32)
-    steps = np.arange(WIDE)
+    numbers = jnp.arange(NX)
+    signed = jnp.where(numbers <= NX // 2, numbers, numbers - NX).astype(jnp.float32)
+    steps = jnp.arange(WIDE)
     rows = CUT * (16 * (pen // 16) + pen % 4) + (4 * CUT * (steps // CUT) + steps % CUT)
     mode = jnp.where(rows <= NZ // 2, rows, rows - NZ).astype(jnp.float32)
     ksquare = mode[:, None] ** 2 + signed[None, :] ** 2
@@ -364,10 +364,11 @@
         grid=(1,),
         in_specs=[whole, last],
         out_specs=pl.BlockSpec((4, 72, TILE), lambda i: (0, 0, 0)),
-        out_shape=f32(4, 72, TILE),
+        out_shape=f32(4, 72, TILE) if INTERPRET else pltpu.VMEM((4, 72, TILE), jnp.float32),
         compiler_params=pltpu.CompilerParams(vmem_limit_bytes=24 << 20),
         interpret=INTERPRET,
     )(*inputs)
+    packed, inverse, damping = lax.optimization_barrier((packed, inverse, damping))
     packed = exchange(packed, axis_index_groups=PEERS)
     both = (f32(TEAM, 144, TILE), f32(2, WIDE, NX))
     send, fields = call(

time: 126 us -> 125 us (level)
  blocking collectives: 69.6 us -> 89.4 us
  starting transfers between devices: 20.3 us -> 10 us
  waiting for transfers between devices: 22.7 us -> 14 us
  Pallas kernels: 11.8 us -> 10.4 us
    all_to_all x0 -> x1, blocking collectives: none -> 19.7 us  [body(): packed = exchange(packed, axis_index_groups=PEERS)]
    all_to_all x1 -> x0, starting transfers between devices: 10.3 us -> none  [body(): packed = exchange(packed, axis_index_groups=PEERS)]
    all_to_all x1 -> x0, waiting for transfers between devices: 9.47 us -> none  [body(): packed = exchange(packed, axis_index_groups=PEERS)]
  transfers between devices with their start and end apart: 4 -> 3, of which waited for: 4 -> 3; matrix products, arithmetic and copies ran while one was open for 0% -> 0% of each run, Pallas kernels for 2% -> 1%
where the time goes in v3:
time: 125 us
  blocking collectives  89.4 us (72%)
  waiting for transfers between devices  14 us (11%)
  Pallas kernels  10.4 us (8%)
  starting transfers between devices  10 us (8%)
    all_to_all x2, blocking collectives, body(): recv = exchange(send, axis_index_groups=TEAMS)  24.5 us
    all_to_all x1, blocking collectives, body(): packed = exchange(packed, axis_index_groups=PEERS)  19.7 us
    all_to_all x2, blocking collectives, body(): recv = exchange(modes, axis_index_groups=TEAMS)  17 us
    all_to_all x1, blocking collectives, body(): sums = everywhere(sums, axis_index_groups=planes)  16.4 us
    all_to_all x1, blocking collectives, body(): ends = exchange(ends, axis_index_groups=PEERS)  11.8 us
    pallas_call x8, Pallas kernels, call(): pl.pallas_call(kernel, in_specs=[vmem] * len(operands), out_specs=[vmem]...  9.31 us
    all_to_all x1, waiting for transfers between devices, body(): sums = everywhere(partial, axis_index_groups=columns)  5.72 us
    ppermute x1, starting transfers between devices, body(): tangent = lax.ppermute(ends[:, 36:72].reshape(144, TILE), 'seg', ring)  4.51 us
  transfers between devices with their start and end apart: 3, of which 3 were waited for; matrix products, arithmetic and copies ran while one was open for 0% of the time, Pallas kernels for 1%

profile of v3, /device:TPU:8, one launch (start us, length us, event | category | flops | bytes accessed | tf_op | source)
XLA Modules:
  0.0 124.9 jit_solution(16079697306147872557)
XLA Ops:
  0.6 0.0 copy-start.1
  0.7 0.1 fusion.3
  0.8 1.1 shard_map.76
  1.9 19.7 %all_to_all.40.recv_ref = f32[4,72,128]{2,1,0:T(8,128)S(1)} all-to-all(f32[4,72,128]{2,1,0:T(8,128)S(1)} %shard_map.76), channel_id=1, replica_groups={{0,4,8,12},{1,5,9,13},{2,6,10,14},{3,7,11,15},{16,20,24,28},{17,21,25,2..., dimensions={0} | all-to-all | bytes 294912 | tf_op jit(solution)/shard_map/all_to_all | solution.py:372
  21.6 0.0 copy-done.1
  21.6 1.0 shard_map.77
  22.6 0.0 copy-start.3
  22.6 0.0 copy-start.4
  22.6 12.2 %all_to_all.41.recv_ref = f32[8,144,128]{2,1,0:T(8,128)S(1)} all-to-all(f32[8,144,128]{2,1,0:T(8,128)S(1)} %get-tuple-element.21), channel_id=1, replica_groups={{0,1,2,3,16,17,18,19},{4,5,6,7,20,21,22,23},{8,9,10,11,24,25,26,27},{12..., dimensions={0} | all-to-all | bytes 1179648 | tf_op jit(solution)/shard_map/all_to_all | solution.py:378
  34.8 0.0 copy-done.3
  34.8 0.0 copy-done.4
  34.8 1.4 %shard_map.78 = f32[8,48,128]{2,1,0:T(8,128)S(1)} custom-call(f32[8,144,128]{2,1,0:T(8,128)S(1)} %all_to_all.41.recv_ref, bf16[768,384]{1,0:T(8,128)(2,1)S(1)} %copy-done.3, bf16[768,384]{1,0:T(8,128)(2,1)S(1)} %copy-done.4), custom_call_target="tpu_custom_call" | custom-call | flops 900000000 | bytes 2500000 | tf_op jit(solution)/shard_map/pallas_call | solution.py:108
  36.2 8.5 %all_to_all.42.recv_ref = f32[8,48,128]{2,1,0:T(8,128)S(1)} all-to-all(f32[8,48,128]{2,1,0:T(8,128)S(1)} %shard_map.78), channel_id=1, replica_groups={{0,1,2,3,16,17,18,19},{4,5,6,7,20,21,22,23},{8,9,10,11,24,25,26,27},{12..., dimensions={0} | all-to-all | bytes 393216 | tf_op jit(solution)/shard_map/all_to_all | solution.py:386
  44.8 1.3 %shard_map.79 = (f32[8,144,128]{2,1,0:T(8,128)S(1)}, f32[2,48,384]{2,1,0:T(8,128)S(1)}) custom-call(f32[8,48,128]{2,1,0:T(8,128)S(1)} %all_to_all.42.recv_ref, f32[2,48,384]{2,1,0:T(8,128)S(1)} %get-tuple-element.22.old_ref, f32[48,384]{1,0:T(8,128)S(1)} %get-tuple-element.23.damping_ref, f32[48,384]{1,0:T(8,128)S(1)} %get-tuple-element.20.inverse_ref, ...), custom_call_target="tpu_custom_call" | custom-call | flops 900000000 | bytes 3000000 | tf_op jit(solution)/shard_map/pallas_call | solution.py:108
  46.1 12.3 %all_to_all.43.recv_ref = f32[8,144,128]{2,1,0:T(8,128)S(1)} all-to-all(f32[8,144,128]{2,1,0:T(8,128)S(1)} %get-tuple-element.24), channel_id=1, replica_groups={{0,1,2,3,16,17,18,19},{4,5,6,7,20,21,22,23},{8,9,10,11,24,25,26,27},{12..., dimensions={0} | all-to-all | bytes 1179648 | tf_op jit(solution)/shard_map/all_to_all | solution.py:378
  58.3 1.5 %shard_map.80 = f32[8,48,128]{2,1,0:T(8,128)S(1)} custom-call(f32[8,144,128]{2,1,0:T(8,128)S(1)} %all_to_all.43.recv_ref, bf16[768,384]{1,0:T(8,128)(2,1)S(1)} %copy-done.3, bf16[768,384]{1,0:T(8,128)(2,1)S(1)} %copy-done.4), custom_call_target="tpu_custom_call" | custom-call | flops 900000000 | bytes 2500000 | tf_op jit(solution)/shard_map/pallas_call | solution.py:108
  59.8 8.5 %all_to_all.44.recv_ref = f32[8,48,128]{2,1,0:T(8,128)S(1)} all-to-all(f32[8,48,128]{2,1,0:T(8,128)S(1)} %shard_map.80), channel_id=1, replica_groups={{0,1,2,3,16,17,18,19},{4,5,6,7,20,21,22,23},{8,9,10,11,24,25,26,27},{12..., dimensions={0} | all-to-all | bytes 393216 | tf_op jit(solution)/shard_map/all_to_all | solution.py:386
  68.3 0.0 copy-start
  68.3 0.4 shard_map.81
  68.7 11.8 %all_to_all.45 = f32[4,72,128]{2,1,0:T(8,128)S(1)} all-to-all(f32[4,72,128]{2,1,0:T(8,128)S(1)} %shard_map.81), channel_id=1, replica_groups={{0,4,8,12},{1,5,9,13},{2,6,10,14},{3,7,11,15},{16,20,24,28},{17,21,25,2..., dimensions={0} | all-to-all | bytes 294912 | tf_op jit(solution)/shard_map/all_to_all | solution.py:402
  80.5 4.5 %collective-permute-start = (f32[144,128]{1,0:T(8,128)S(1)}, f32[144,128]{1,0:T(8,128)S(1)}, u32[]{:S(2)}, u32[]{:S(2)}) collective-permute-start(f32[144,128]{1,0:T(8,128)S(1)} %reshape.50), channel_id=1, source_target_pairs={{0,32},{32,64},{64,96},{96,128},{128,160},{160,192},{192,224},{224... | collective-permute-start | bytes 221192 | tf_op jit(solution)/shard_map/ppermute | solution.py:403
  85.0 0.0 copy-done
  85.0 1.6 %shard_map.82.gram_ref = f32[8,128]{1,0:T(8,128)S(1)} custom-call(f32[16,12,4,384]{3,2,1,0:T(4,128)S(1)} %bitcast.5), custom_call_target="tpu_custom_call" | custom-call | flops 10000000 | bytes 1300000 | tf_op jit(solution)/shard_map/pallas_call | solution.py:108
  86.6 0.0 copy-start.2
  86.6 0.1 reshape.51
  86.7 4.4 %collective-permute-done.planes_ref = f32[144,128]{1,0:T(8,128)S(1)} collective-permute-done((f32[144,128]{1,0:T(8,128)S(1)}, f32[144,128]{1,0:T(8,128)S(1)}, u32[]{:S(2)}, u32[]{:S(2)}) %collective-permute-start) | collective-permute-done | bytes 73760 | tf_op jit(solution)/shard_map/ppermute | solution.py:403
  91.1 1.2 shard_map.83
  92.2 3.5 %all-to-all-start.6 = ((f32[16,8,128]{2,1,0:T(8,128)}), f32[16,8,128]{2,1,0:T(8,128)S(1)}, u32[]{:S(2)}, u32[]{:S(2)}) async-start(f32[16,8,128]{2,1,0:T(8,128)} %get-tuple-element.27), calls=%async_computation.6 | async-start | bytes 131072 | tf_op jit(solution)/shard_map/all_to_all | solution.py:422
  95.8 2.0 %collective-permute-start.1 = (f32[144,128]{1,0:T(8,128)S(1)}, f32[144,128]{1,0:T(8,128)S(1)}, u32[]{:S(2)}, u32[]{:S(2)}) collective-permute-start(f32[144,128]{1,0:T(8,128)S(1)} %reshape.51), channel_id=1, source_target_pairs={{0,32},{32,64},{64,96},{96,128},{128,160},{160,192},{192,224},{224... | collective-permute-start | bytes 221192 | tf_op jit(solution)/shard_map/ppermute | solution.py:413
  97.8 5.7 %all-to-all-done.6 = f32[16,8,128]{2,1,0:T(8,128)S(1)} async-done(((f32[16,8,128]{2,1,0:T(8,128)}), f32[16,8,128]{2,1,0:T(8,128)S(1)}, u32[]{:S(2)}, u32[]{:S(2)}) %all-to-all-start.6) | async-done | bytes 65568 | tf_op jit(solution)/shard_map/all_to_all | solution.py:422
  103.5 3.9 %collective-permute-done.1.planes_ref = f32[144,128]{1,0:T(8,128)S(1)} collective-permute-done((f32[144,128]{1,0:T(8,128)S(1)}, f32[144,128]{1,0:T(8,128)S(1)}, u32[]{:S(2)}, u32[]{:S(2)}) %collective-permute-start.1) | collective-permute-done | bytes 73760 | tf_op jit(solution)/shard_map/ppermute | solution.py:413
  107.4 16.4 %all_to_all.46.sums_ref = f32[32,8,128]{2,1,0:T(8,128)S(1)} all-to-all(f32[32,8,128]{2,1,0:T(8,128)S(1)} %broadcast_in_dim.5), channel_id=1, replica_groups={{0,16,32,48,64,80,96,112,128,144,160,176,192,208,224,240,256,272,288,30..., dimensions={0} | all-to-all | bytes 262144 | tf_op jit(solution)/shard_map/all_to_all | solution.py:426
  123.8 0.0 copy-done.2
  123.8 1.0 shard_map.84
  (6 shorter events, 0.1 us)
Async XLA Ops:
  0.6 21.0 %copy-start.1 = (bf16[768,768]{1,0:T(8,128)(2,1)S(1)}, bf16[768,768]{1,0:T(8,128)(2,1)}, u32[]{:S(2)}) copy-start(bf16[768,768]{1,0:T(8,128)(2,1)} %constant.73.clone.table_ref) | copy-start | bytes 3538948
  22.6 12.2 %copy-start.3 = (bf16[768,384]{1,0:T(8,128)(2,1)S(1)}, bf16[768,384]{1,0:T(8,128)(2,1)}, u32[]{:S(2)}) copy-start(bf16[768,384]{1,0:T(8,128)(2,1)} %constant.74.clone.cas_ref) | copy-start | bytes 1769476
  22.6 12.2 %copy-start.4 = (bf16[768,384]{1,0:T(8,128)(2,1)S(1)}, bf16[768,384]{1,0:T(8,128)(2,1)}, u32[]{:S(2)}) copy-start(bf16[768,384]{1,0:T(8,128)(2,1)} %constant.75.clone.slope_ref) | copy-start | bytes 1769476
  68.3 16.7 %copy-start = (f32[16,4,12,384]{3,1,2,0:T(4,128)S(1)}, f32[16,4,12,384]{3,1,2,0:T(4,128)}, u32[]{:S(2)}) copy-start(f32[16,4,12,384]{3,1,2,0:T(4,128)} %param.6) | copy-start | bytes 3538948
  80.5 10.6 %collective-permute-start = (f32[144,128]{1,0:T(8,128)S(1)}, f32[144,128]{1,0:T(8,128)S(1)}, u32[]{:S(2)}, u32[]{:S(2)}) collective-permute-start(f32[144,128]{1,0:T(8,128)S(1)} %reshape.50), channel_id=1, source_target_pairs={{0,32},{32,64},{64,96},{96,128},{128,160},{160,192},{192,224},{224... | collective-permute-start | bytes 221192 | tf_op jit(solution)/shard_map/ppermute | solution.py:403
  86.6 37.2 %copy-start.2 = (f32[4,12,384]{2,0,1:T(4,128)S(1)}, f32[4,12,384]{2,0,1:T(4,128)}, u32[]{:S(2)}) copy-start(f32[4,12,384]{2,0,1:T(4,128)} %param.5) | copy-start | bytes 221188
  92.2 11.3 %all-to-all-start.6 = ((f32[16,8,128]{2,1,0:T(8,128)}), f32[16,8,128]{2,1,0:T(8,128)S(1)}, u32[]{:S(2)}, u32[]{:S(2)}) async-start(f32[16,8,128]{2,1,0:T(8,128)} %get-tuple-element.27), calls=%async_computation.6 | async-start | bytes 131072 | tf_op jit(solution)/shard_map/all_to_all | solution.py:422
  95.8 11.7 %collective-permute-start.1 = (f32[144,128]{1,0:T(8,128)S(1)}, f32[144,128]{1,0:T(8,128)S(1)}, u32[]{:S(2)}, u32[]{:S(2)}) collective-permute-start(f32[144,128]{1,0:T(8,128)S(1)} %reshape.51), channel_id=1, source_target_pairs={{0,32},{32,64},{64,96},{96,128},{128,160},{160,192},{192,224},{224... | collective-permute-start | bytes 221192 | tf_op jit(solution)/shard_map/ppermute | solution.py:413
